TPU v7x, 32 devices: a whole 2x2x4 slice. The times are simulated.
32 devices in a mesh: gx: 4 (over y, core), gy: 4 (over z), frame: 2 (over x).
Axes of the slice: x: 2, y: 2, z: 4, core: 2. Of those that a mesh axis runs over, the one named last changes fastest.
Arguments:
- features: bfloat16 [8, 8, 128, 128], P(('frame', 'gx'), 'gy'), parts along dimension 0, may hold values from -6 to 6
- positions: float32 [8, 8, 3, 128], P(('frame', 'gx'), 'gy'), parts along dimension 0, may hold values from 0 to 1
- bead_types: int32 [8, 8, 128], P(('frame', 'gx'), 'gy'), parts along dimension 0, may hold values from 0 to 15
- cell_counts: int32 [8, 8], P(('frame', 'gx'), 'gy'), parts along dimension 0, may hold values from 48 to 128
- w_value: bfloat16 [128, 128], replicated, may hold values from -0.5 to 0.5
- w_radial: float32 [8, 128], replicated, may hold values from -0.6 to 0.6
- type_gain: float32 [16, 128], replicated, may hold values from 0.1 to 1.9
- w_out: bfloat16 [128, 128], replicated, may hold values from -0.5 to 0.5
- cotangent: bfloat16 [8, 8, 128, 128], P(('frame', 'gx'), 'gy'), parts along dimension 0, may hold values from -6 to 6
Outputs:
- out_feat: bfloat16 [8, 8, 128, 128], P(('frame', 'gx'), 'gy'), parts along dimension 0
- grad_feat: bfloat16 [8, 8, 128, 128], P(('frame', 'gx'), 'gy'), parts along dimension 0
- grad_pos: float32 [8, 8, 3, 128], P(('frame', 'gx'), 'gy'), parts along dimension 0
- grad_wvalue: float32 [256, 128], P('frame'), parts along dimension 0
- grad_wradial: float32 [16, 128], P('frame'), parts along dimension 0
- grad_gain: float32 [32, 128], P('frame'), parts along dimension 0
- grad_wout: float32 [256, 128], P('frame'), parts along dimension 0
There are 2 independent parts, one for each index of `frame`. A program takes and returns all parts, laid end to end along the dimension named above; an argument that names none is the same for every part. Nothing has to cross between parts.
All inputs are finite; a program needn't handle non-finite values.
Results may differ from a plain program's by a relative error of at most 0.012.
Values may be sent and summed in bfloat16 or wider, within the bound.
No kernel may reach another device: no remote copies, remote signals or barrier semaphores. Data moves between devices by JAX's collectives and lax.ppermute only.
A program may use at most 64 MiB of HBM per device.

v0:
```python
import functools
import math

import jax
import jax.numpy as jnp
from jax import lax
from jax.experimental import pallas as pl
from jax.experimental.pallas import tpu as pltpu
from jax.sharding import PartitionSpec as P


HZ = 6
SOFTEN = 0.01
FAR = 1024.0
AUX = 8
LINES = 16
STRIP = 32
LANES = 128
LOG2E = math.log2(math.e)


f32 = jnp.float32
bf16 = jnp.bfloat16


def split3(x):
    hi = x.astype(bf16)
    rest = x - hi.astype(f32)
    mid = rest.astype(bf16)
    low = (rest - mid.astype(f32)).astype(bf16)
    return hi, mid, low


def dot(a, b):
    return jnp.dot(a, b, preferred_element_type=f32)


def dot_t(a, b):
    return lax.dot_general(a, b, (((1,), (1,)), ((), ())), preferred_element_type=f32)


def identity(size):
    rows = lax.broadcasted_iota(jnp.int32, (size, size), 0)
    lanes = lax.broadcasted_iota(jnp.int32, (size, size), 1)
    return jnp.where(rows == lanes, 1.0, 0.0).astype(bf16)


def gain_columns(type_gain):
    parts = [part.astype(f32) for part in split3(type_gain[...])]
    count, channels = type_gain.shape
    rows = jnp.concatenate(parts + [jnp.zeros((channels - 3 * count, channels), f32)], axis=0)
    return rows.T[:, 0 : 3 * count].astype(bf16)


def onehot_rows(types_row, type_count, slots):
    rows = lax.broadcasted_iota(jnp.int32, (3 * type_count, slots), 0)
    hit = (rows == types_row) | (rows == types_row + type_count) | (rows == types_row + 2 * type_count)
    return jnp.where(hit, 1.0, 0.0).astype(bf16)


def pack_kernel(order, counts, feat, pos, types, packed, counts_here, pos_here, types_here, sems):
    slots = feat.shape[2]
    moves = [(counts, counts_here), (pos, pos_here), (types, types_here)]
    for place in range(2):
        cell = jnp.where(order[1] == 0, place, 1 - place)
        moves.append((feat.at[0, cell], packed.at[place, 0:slots, :]))
    copies = [pltpu.make_async_copy(a, b, sems.at[i]) for i, (a, b) in enumerate(moves)]
    for copy in copies:
        copy.start()
    for copy in copies[:3]:
        copy.wait()
    for place in range(2):
        cell = jnp.where(order[1] == 0, place, 1 - place)
        lane = lax.broadcasted_iota(jnp.int32, (1, slots), 1)
        valid = lane < counts_here[0, cell]
        parts = [[], []]
        for comp in range(3):
            row = pos_here[0, comp, pl.ds(cell, 1), :]
            if comp == 2:
                row = row * float(HZ)
            row = jnp.where(valid, row, -FAR)
            for which, part in enumerate(split3(row)[:2]):
                parts[which].append(part.astype(f32))
        rows = parts[0] + parts[1]
        rows.append(types_here[0, pl.ds(cell, 1), :].astype(f32))
        rows.append(jnp.zeros((AUX - len(rows), slots), f32))
        packed[place, slots : slots + AUX, :] = jnp.concatenate(rows, axis=0).astype(bf16)
    for copy in copies[3:]:
        copy.wait()


def load_kernel(*refs):
    sources, targets, sems = refs[:5], refs[5:10], refs[10]
    copies = [pltpu.make_async_copy(a, b, sems.at[i]) for i, (a, b) in enumerate(zip(sources, targets))]
    for copy in copies:
        copy.start()
    for copy in copies:
        copy.wait()


def pair_terms(near_pos, index, own_xyz, is_self, first_row, basis_count):
    n1 = float(basis_count - 1)
    gamma = 0.5 * n1 * n1
    delta = [near_pos[index, comp : comp + 1, :] - own_xyz[comp] for comp in range(3)]
    dist_sq = delta[0] * delta[0] + delta[1] * delta[1] + delta[2] * delta[2]
    dist_sq = jnp.minimum(dist_sq, 1.0)
    inside = 1.0 - dist_sq
    radius_sq = dist_sq + SOFTEN
    inverse = lax.rsqrt(radius_sq)
    radius = radius_sq * inverse
    gauss = jnp.exp2(radius_sq * (-gamma * LOG2E))
    step = jnp.exp2(radius * (n1 * LOG2E))
    if is_self:
        rows = first_row + lax.broadcasted_iota(jnp.int32, gauss.shape, 0)
        lanes = lax.broadcasted_iota(jnp.int32, gauss.shape, 1)
        gauss = jnp.where(rows == lanes, 0.0, gauss)
    part = inside * gauss
    weight = inside * part
    value_factor = part * (inside * -n1 - 2.0 * n1 / gamma)
    slope_factor = weight * (inverse * step)
    return step, weight, value_factor, slope_factor


def near_cell(aux, row, col, order):
    sx = jnp.where(order[0] == 0, 1.0, -1.0).astype(f32)
    sy = jnp.where(order[1] == 0, 1.0, -1.0).astype(f32)
    aux = aux.astype(f32)
    xyz = aux[0:3] + aux[3:6]
    x = xyz[0:1] + sx * float(1 - row)
    y = xyz[1:2] + sy * float(col)
    return [x, y, xyz[2:3]], xyz[0:1] < -0.5 * FAR, aux[6:7].astype(jnp.int32)


def strip_of(s):
    first = pl.multiple_of(s * STRIP, STRIP)
    return first, pl.ds(first, STRIP)


def stage(count, *steps):
    def body(s, carry):
        for step in steps:
            step(s)
        return carry

    lax.fori_loop(0, count, body, 0)


def fill_pairs(basis_count, slots, near_pos, own_pos, place, self_block, terms, weights, s):
    first, strip = strip_of(s)
    own_xyz = [own_pos[place, comp, strip, :] for comp in range(3)]
    for block in range(weights.shape[1] // slots):
        there = slice(block * slots, (block + 1) * slots)
        step, weight, value_factor, slope_factor = pair_terms(
            near_pos, block, own_xyz, block == self_block, first, basis_count
        )
        terms[0, strip, there] = step
        terms[1, strip, there] = value_factor
        terms[2, strip, there] = slope_factor
        for k in range(basis_count):
            rows = pl.ds(pl.multiple_of(first + k * slots, STRIP), STRIP)
            weights[rows, there] = weight.astype(bf16)
            if k < basis_count - 1:
                weight = weight * step


def carry_values(slots, value_t, gain_t, eye, near, here):
    near_feat, near_val, carried_t, onehot, projected, gains = near
    proj = dot_t(value_t, near_feat[here, :])
    gain = dot(gain_t, onehot[:, here])
    projected[:, here] = proj
    gains[:, here] = gain
    carried = (proj * gain).astype(bf16)
    carried_t[:, here] = carried
    for first in range(here.start, here.stop, slots):
        there = slice(first - here.start, first - here.start + slots)
        near_val[first : first + slots, :] = dot_t(eye, carried[:, there]).astype(bf16)


def chunk_of(s, size):
    return pl.ds(pl.multiple_of(s * size, size), size)


def early_kernel(
    basis_count, order, own, row_a, row_b, w_value, w_radial, type_gain,
    near_pos, own_pos, near_feat, near_val, carried_t, onehot, projected, gains,
    weights_b, weights_a, terms_b, terms_a, summed_b, summed_a, columns, value_t, gain_t,
):
    slots = near_feat.shape[1]
    strips = slots // STRIP
    chunk = basis_count * slots // strips
    weights, terms, summed = (weights_b, weights_a), (terms_b, terms_a), (summed_b, summed_a)
    for index in range(6):
        col, row = index // 3 + 1, index % 3
        ref = (row_a, own, row_b)[row]
        here = slice(index * slots, (index + 1) * slots)
        near_feat[here, :] = ref[col - 1, 0:slots, :]
        xyz, unused, types = near_cell(ref[col - 1, slots : slots + AUX, :], row, col, order)
        onehot[:, here] = onehot_rows(types, type_gain.shape[0], slots)
        for comp in range(3):
            near_pos[index, comp : comp + 1, :] = xyz[comp]
            if row == 1:
                line = jnp.where(unused, FAR, xyz[comp])
                own_pos[col - 1, comp] = jnp.broadcast_to(line, (slots, slots)).T
    near = (near_feat, near_val, carried_t, onehot, projected, gains)
    value_t[...] = w_value[...].astype(f32).T.astype(bf16)
    gain_t[...] = gain_columns(type_gain)
    carry_values(slots, value_t[...], gain_t[...], identity(slots), near, slice(0, 6 * slots))
    channels = w_value.shape[0]
    radial = [w_radial[k : k + 1, :] * math.exp(-0.5 * k * k) for k in range(basis_count)]
    radial_t = jnp.concatenate(radial + [jnp.zeros((channels - basis_count, channels), f32)], axis=0).T
    for k in range(basis_count):
        columns[k] = jnp.broadcast_to(radial_t[:, k : k + 1], (channels, slots))

    def sums(place, s):
        rows = chunk_of(s, chunk)
        summed[place][:, rows] = dot_t(carried_t[...], weights[place][rows, :])

    def pairs(place, s):
        fill_pairs(
            basis_count, slots, near_pos, own_pos, place, 3 * place + 1, terms[place], weights[place], s
        )

    run = functools.partial
    stage(strips, run(pairs, 0))
    stage(strips, run(sums, 0), run(pairs, 1))
    stage(strips, run(sums, 1))


def main_kernel(
    basis_count, order, col_a, col_b, cotangent, w_radial, w_out, columns, value_t, gain_t,
    own_pos, in_feat, in_carried_t, in_onehot, in_projected, in_gains,
    in_weights_b, in_weights_a, in_summed_b, in_summed_a,
    out_here, keep, pay_a, pay_b, fold_a, fold_b, own_acc,
    out_pos, ot_val, ot_terms_b, ot_terms_a, grad_agg,
    ot_feat, ot_carried_t, ot_onehot, ot_projected, ot_gains, products, whole,
    ot_weights_b, ot_weights_a, summed_b, summed_a, scaled_tb, scaled_ta, in_back, ot_back,
):
    slots, channels = cotangent.shape[2], cotangent.shape[3]
    type_count = gain_t.shape[1] // 3
    third = 3 * slots
    strips = slots // STRIP
    chunk = basis_count * slots // strips
    in_weights, ot_weights = (in_weights_b, in_weights_a), (ot_weights_b, ot_weights_a)
    ot_terms = (ot_terms_b, ot_terms_a)
    in_summed, summed = (in_summed_b, in_summed_a), (summed_b, summed_a)
    scaled_t = (scaled_tb, scaled_ta)
    for index in range(6):
        place, row = index // 3, index % 3
        ref = (col_b, col_a)[place]
        here = slice(index * slots, (index + 1) * slots)
        ot_feat[here, :] = ref[row, 0:slots, :]
        xyz, _, types = near_cell(ref[row, slots : slots + AUX, :], row, 3 * place, order)
        ot_onehot[:, here] = onehot_rows(types, type_count, slots)
        for comp in range(3):
            out_pos[index, comp : comp + 1, :] = xyz[comp]
    scale = [math.exp(-0.5 * k * k) for k in range(basis_count)]
    near = (ot_feat, ot_val, ot_carried_t, ot_onehot, ot_projected, ot_gains)
    carry_values(slots, value_t[...], gain_t[...], identity(slots), near, slice(0, 6 * slots))

    def outer(place):
        return slice(place * third, (place + 1) * third)

    def pairs(place, s):
        cells = out_pos.at[place * 3 : place * 3 + 3]
        fill_pairs(basis_count, slots, cells, own_pos, place, -1, ot_terms[place], ot_weights[place], s)

    def sums(place, s):
        rows = chunk_of(s, chunk)
        summed[place][:, rows] = in_summed[place][:, rows] + dot_t(
            ot_carried_t[:, outer(place)], ot_weights[place][rows, :]
        )

    def epilogue(place):
        aggregate_t = None
        for k in range(basis_count):
            term = summed[place][:, k * slots : (k + 1) * slots] * columns[k]
            aggregate_t = term if aggregate_t is None else aggregate_t + term
        agg_half = aggregate_t.T.astype(bf16)
        cell = jnp.where(order[1] == 0, place, 1 - place)
        pre_act = dot(agg_half, w_out[...])
        sig = jax.nn.sigmoid(pre_act)
        center = in_feat[(3 * place + 1) * slots : (3 * place + 2) * slots, :]
        out_here[place] = (center.astype(f32) + pre_act * sig).astype(bf16)
        grad_pre = (
            cotangent[0, cell].astype(f32) * sig * (1.0 + pre_act * (1.0 - sig))
        ).astype(bf16)
        agg_half = dot_t(grad_pre, w_out[...]).astype(bf16)
        grad_agg[place] = agg_half
        agg_t = agg_half.astype(f32).T
        for k in range(basis_count):
            here = slice(k * slots, (k + 1) * slots)
            scaled_t[place][:, here] = (agg_t * columns[k]).astype(bf16)
            product = agg_t * summed[place][:, here]
            products[:, here] = product if place == 0 else products[:, here] + product
        return dot(aggregate_t.astype(bf16), grad_pre)

    def value_grads(place):
        inner = dot(scaled_t[place][...], in_weights[place][...])
        in_back[...] = inner if place == 0 else in_back[...] + inner
        ot_back[:, outer(place)] = dot(scaled_t[place][...], ot_weights[place][...])

    run = functools.partial
    stage(strips, run(pairs, 0))
    stage(strips, run(sums, 0), run(pairs, 1))
    for s in range(strips):
        sums(1, s)
    wout = epilogue(0)
    value_grads(0)
    wout = wout + epilogue(1)
    value_grads(1)

    wvalue = ggain = None
    for back, feat, onehot, projected, gains in (
        (in_back, in_feat, in_onehot, in_projected, in_gains),
        (ot_back, ot_feat, ot_onehot, ot_projected, ot_gains),
    ):
        half = (back[...] * gains[...]).astype(bf16)
        wvalue_part = dot(half, feat[...])
        ggain_part = dot_t((back[...] * projected[...]).astype(bf16), onehot[0:type_count, :])
        wvalue = wvalue_part if wvalue is None else wvalue + wvalue_part
        ggain = ggain_part if ggain is None else ggain + ggain_part
    ggain = jnp.concatenate([ggain, jnp.zeros((channels, slots - ggain.shape[1]), f32)], axis=1).T
    group = lax.broadcasted_iota(jnp.int32, (basis_count, basis_count * slots), 1) // slots
    mine = lax.broadcasted_iota(jnp.int32, (basis_count, basis_count * slots), 0)
    select = jnp.where(group == mine, 1.0, 0.0).astype(bf16)
    wradial = dot_t(select, products[...].astype(bf16))
    wradial = jnp.concatenate([wradial[k : k + 1] * scale[k] for k in range(basis_count)], axis=0)
    pad = 2 * keep.shape[0] - 2 * channels - type_count - basis_count
    tail = [ggain[0:type_count], wradial] + ([jnp.zeros((pad, channels), f32)] if pad else [])
    full = jnp.concatenate([wvalue.T, wout] + tail, axis=0).astype(bf16)
    rows = keep.shape[0]
    whole[0] = full[0:rows]
    whole[1] = full[rows : 2 * rows]
    keep[...] = whole[order[0]]
    for ref in (pay_a, pay_b):
        ref[0:rows, :] = whole[1 - order[0]]
    for col in range(4):
        for row in range(3):
            inner = col in (1, 2)
            local = (col - 1) * 3 + row if inner else (0 if col == 0 else 3) + row
            back = (in_back if inner else ot_back)[:, local * slots : (local + 1) * slots]
            if row == 1:
                own_acc[col] = back
            elif inner:
                ref = fold_a if row == 0 else fold_b
                ref[(col - 1) * slots : col * slots, :] = back.astype(bf16)
            else:
                ref = pay_a if row == 0 else pay_b
                base = rows + (0 if col == 0 else slots)
                ref[base : base + slots, :] = back.astype(bf16)


def pulls_kernel(
    basis_count, order, in_pos, own_pos, in_val, in_terms_b, in_terms_a, out_pos, ot_val,
    ot_terms_b, ot_terms_a, grad_agg, w_radial,
    lines,
    scaled_b, scaled_a, in_grad_b, in_grad_a, ot_grad_b, ot_grad_a, pull_own, pull_far,
):
    slots = in_pos.shape[2]
    third = 3 * slots
    strips = slots // STRIP
    chunk = basis_count * slots // strips
    in_terms, ot_terms = (in_terms_b, in_terms_a), (ot_terms_b, ot_terms_a)
    scaled = (scaled_b, scaled_a)
    in_grad, ot_grad = (in_grad_b, in_grad_a), (ot_grad_b, ot_grad_a)

    def weight_grads(place, s):
        rows = chunk_of(s, chunk)
        in_grad[place][rows, :] = dot_t(scaled[place][rows, :], in_val[...])
        outer = slice(place * third, (place + 1) * third)
        ot_grad[place][rows, :] = dot_t(scaled[place][rows, :], ot_val[outer, :])

    def pulls(place, s):
        first, strip = strip_of(s)
        own_xyz = [own_pos[place, comp, strip, :] for comp in range(3)]
        total = [jnp.zeros((STRIP, slots), f32) for _ in range(3)]
        for block in range(9):
            inner = block < 6
            grad = (in_grad if inner else ot_grad)[place]
            terms = (in_terms if inner else ot_terms)[place]
            cells = in_pos if inner else out_pos
            cell = block if inner else place * 3 + block - 6
            index = block if inner else 6 + cell
            local = block if inner else block - 6
            there = slice(local * slots, (local + 1) * slots)

            def grad_of(k):
                rows = pl.ds(pl.multiple_of(first + k * slots, STRIP), STRIP)
                return grad[rows, there]

            step = terms[0, strip, there]
            value = grad_of(basis_count - 1)
            slope = None
            for k in range(basis_count - 2, -1, -1):
                slope = value if slope is None else value + step * slope
                value = grad_of(k) + step * value
            pull = terms[1, strip, there] * value + terms[2, strip, there] * slope
            for comp in range(3):
                force = pull * (cells[cell, comp : comp + 1, :] - own_xyz[comp])
                total[comp] = total[comp] + force
                pull_far[index, comp] += (force[0:8] + force[8:16]) + (force[16:24] + force[24:32])
        for comp in range(3):
            pull_own[place, comp, strip, :] = total[comp]

    run = functools.partial
    pull_far[...] = jnp.zeros_like(pull_far)
    for place in range(2):
        agg = grad_agg[place].astype(f32)
        for k in range(basis_count):
            factor = w_radial[k : k + 1, :] * math.exp(-0.5 * k * k)
            scaled[place][k * slots : (k + 1) * slots, :] = (agg * factor).astype(bf16)
        if place == 0:
            for s in range(strips):
                weight_grads(0, s)
    stage(strips, run(weight_grads, 1), run(pulls, 0))
    stage(strips, run(pulls, 1))
    force = float(basis_count - 1)
    rows = []
    for col in range(4):
        for row in range(3):
            inner = col in (1, 2)
            local = (col - 1) * 3 + row if inner else 6 + (0 if col == 0 else 3) + row
            for comp in range(3):
                line = jnp.sum(pull_far[local, comp], axis=0, keepdims=True)
                if row == 1 and inner:
                    line = line - jnp.sum(pull_own[col - 1, comp].T, axis=0, keepdims=True)
                rows.append(line * (force * HZ if comp == 2 else force))
            rows.append(jnp.zeros((1, slots), f32))
        rows.append(jnp.zeros((4, slots), f32))
    lines[...] = jnp.concatenate(rows, axis=0)


def cells_kernel(
    order, own, got_a, got_b, far, near, lines, cotangent, w_value, gains, grad_feat, grad_pos
):
    slots = own.shape[2]
    for place in range(2):
        cell = jnp.where(order[1] == 0, place, 1 - place)
        here = slice(place * slots, (place + 1) * slots)
        got = far[0:slots, :] if place == 0 else near[near.shape[0] - LINES - slots : near.shape[0] - LINES, :]
        total = own[place + 1] + add(got_a[here, :], got_b[here, :]) + got.astype(f32)
        half = (total * gains[:, (3 * place + 1) * slots : (3 * place + 2) * slots]).astype(bf16)
        grad_feat[0, cell] = (cotangent[0, cell].astype(f32) + dot(w_value[...], half).T).astype(bf16)
        pos = lines[4 * place : 4 * place + 4, :]
        for comp in range(3):
            grad_pos[0, comp, pl.ds(cell, 1), :] = pos[comp : comp + 1]


def emit_kernel(order, out_here, out_feat):
    for place in range(2):
        out_feat[0, jnp.where(order[1] == 0, place, 1 - place)] = out_here[place]


def finish_kernel(order, mine, other, feat, pos, grad_feat, grad_pos, wvalue, wradial, ggain, wout):
    grad_feat[...] = feat[...]
    grad_pos[...] = pos[...]
    first = order[0] == 0
    low = jnp.where(first, mine[...], other[...])
    high = jnp.where(first, other[...], mine[...])
    total = jnp.concatenate([low, high], axis=0)
    base = 0
    for ref in (wvalue, wout, ggain, wradial):
        ref[...] = total[base : base + ref.shape[0]]
        base += ref.shape[0]


def edges(axis):
    count = lax.axis_size(axis)
    assert count % 2 == 0 and count > 2 and count & (count - 1) == 0
    even = [(i, i ^ 1) for i in range(count)]
    odd = [(i, (i + 1) % count if i % 2 else (i - 1) % count) for i in range(count)]
    return even, odd


def across(axis, step):
    return [(i, i ^ step) for i in range(lax.axis_size(axis))]


def add(a, b):
    return a.astype(f32) + b.astype(f32)


def on_device(
    features, positions, bead_types, cell_counts, w_value, w_radial, type_gain, w_out, cotangent
):
    row_count, col_count, slots, channels = features.shape
    basis_count, type_count = w_radial.shape[0], type_gain.shape[0]
    assert row_count == 1 and col_count == 2 and slots == channels == LANES
    assert 3 * type_count <= slots and type_count % 8 == 0 and basis_count == 8
    order = jnp.stack([lax.axis_index("gx") % 2, lax.axis_index("gy") % 2]).astype(jnp.int32)
    smem = pl.BlockSpec(memory_space=pltpu.SMEM)
    vmem = pl.BlockSpec(memory_space=pltpu.VMEM)
    x_even, x_odd = edges("gx")
    y_even, y_odd = edges("gy")
    size = slots + AUX
    inner, outer, tall = 6 * slots, 3 * slots, basis_count * slots
    rows = -(-(2 * channels + type_count + basis_count) // 32) * 16
    kinds = 3 * type_count
    shape = jax.ShapeDtypeStruct

    def call(kernel, mib, out_shape, arrays, scratch=()):
        return pl.pallas_call(
            kernel,
            out_shape=out_shape,
            in_specs=[smem] + [vmem] * len(arrays),
            out_specs=jax.tree.map(lambda _: vmem, out_shape),
            scratch_shapes=list(scratch),
            compiler_params=pltpu.CompilerParams(vmem_limit_bytes=mib * 2**20),
        )(order, *arrays)

    hbm = pl.BlockSpec(memory_space=pltpu.HBM)
    small = pltpu.CompilerParams(vmem_limit_bytes=4 * 2**20)

    def in_hbm(*arrays):
        return [pltpu.with_memory_space_constraint(a, pltpu.HBM) for a in arrays]

    packed = pl.pallas_call(
        pack_kernel,
        out_shape=shape((2, size, channels), bf16),
        in_specs=[smem] + [hbm] * 4,
        out_specs=vmem,
        scratch_shapes=[
            pltpu.SMEM(cell_counts.shape, jnp.int32),
            pltpu.VMEM((row_count, 3, col_count, slots), f32),
            pltpu.VMEM(bead_types.shape, jnp.int32),
            pltpu.SemaphoreType.DMA((5,)),
        ],
        compiler_params=small,
        name="pack",
    )(order, *in_hbm(cell_counts, features, jnp.swapaxes(positions, 1, 2), bead_types))
    later = (cotangent, w_value, w_radial, type_gain, w_out)
    cotangent, w_value, w_radial, type_gain, w_out = pl.pallas_call(
        load_kernel,
        out_shape=tuple(shape(a.shape, a.dtype) for a in later),
        in_specs=[hbm] * 5,
        out_specs=(vmem,) * 5,
        scratch_shapes=[pltpu.SemaphoreType.DMA((5,))],
        compiler_params=small,
        name="load",
    )(*in_hbm(*later))
    row_b = lax.ppermute(packed, "gx", x_odd)
    row_a = lax.ppermute(packed, "gx", x_even)
    col_b = lax.ppermute(jnp.stack([row_a[0], packed[0], row_b[0]]), "gy", y_odd)
    col_a = lax.ppermute(jnp.stack([row_a[1], packed[1], row_b[1]]), "gy", y_even)
    early = call(
        functools.partial(early_kernel, basis_count), 8,
        (
            shape((6, 8, slots), f32),
            shape((2, 3, slots, slots), f32),
            shape((inner, channels), bf16),
            shape((inner, channels), bf16),
            shape((channels, inner), bf16),
            shape((kinds, inner), bf16),
            shape((channels, inner), f32),
            shape((channels, inner), f32),
        )
        + (shape((tall, inner), bf16),) * 2
        + (shape((3, slots, inner), f32),) * 2
        + (shape((channels, tall), f32),) * 2
        + (
            shape((basis_count, channels, slots), f32),
            shape((channels, channels), bf16),
            shape((channels, kinds), bf16),
        ),
        (packed, row_a, row_b, w_value, w_radial, type_gain),
    )
    (
        in_pos, own_pos, in_feat, in_val, in_carried_t, in_onehot, in_projected, in_gains,
        in_weights_b, in_weights_a, in_terms_b, in_terms_a, in_summed_b, in_summed_a,
        columns, value_t, gain_t,
    ) = early
    (
        out_here, keep, pay_a, pay_b, fold_a, fold_b, own_acc,
        out_pos, ot_val, ot_terms_b, ot_terms_a, grad_agg,
    ) = call(
        functools.partial(main_kernel, basis_count), 16,
        (
            shape((2, slots, channels), bf16),
            shape((rows, channels), bf16),
            shape((rows + 2 * channels, slots), bf16),
            shape((rows + 2 * channels, slots), bf16),
            shape((2 * channels, slots), bf16),
            shape((2 * channels, slots), bf16),
            shape((4, channels, slots), f32),
            shape((6, 8, slots), f32),
            shape((2 * outer, channels), bf16),
        )
        + (shape((3, slots, outer), f32),) * 2
        + (shape((2, slots, channels), bf16),),
        (
            col_a, col_b, cotangent, w_radial, w_out, columns, value_t, gain_t,
            own_pos, in_feat, in_carried_t, in_onehot, in_projected, in_gains,
            in_weights_b, in_weights_a, in_summed_b, in_summed_a,
        ),
        [
            pltpu.VMEM((2 * outer, channels), bf16),
            pltpu.VMEM((channels, 2 * outer), bf16),
            pltpu.VMEM((kinds, 2 * outer), bf16),
            pltpu.VMEM((channels, 2 * outer), f32),
            pltpu.VMEM((channels, 2 * outer), f32),
            pltpu.VMEM((channels, tall), f32),
            pltpu.VMEM((2, rows, channels), bf16),
        ]
        + [pltpu.VMEM((tall, outer), bf16)] * 2
        + [pltpu.VMEM((channels, tall), f32)] * 2
        + [pltpu.VMEM((channels, tall), bf16)] * 2
        + [pltpu.VMEM((channels, inner), f32), pltpu.VMEM((channels, 2 * outer), f32)],
    )
    got_b = lax.ppermute(pay_b, "gx", x_odd)
    got_a = lax.ppermute(pay_a, "gx", x_even)
    if len(x_even) == 4:
        other = lax.ppermute(keep, "gx", across("gx", 2))
        total = add(keep, got_a[:rows]) + add(other, got_b[:rows])
    else:
        total = add(keep, got_a[:rows])
        step = 2
        while step < len(x_even):
            part = total.astype(bf16)
            total = add(part, lax.ppermute(part, "gx", across("gx", step)))
            step *= 2
    lines = call(
        functools.partial(pulls_kernel, basis_count), 20, shape((4 * LINES, slots), f32),
        (
            in_pos, own_pos, in_val, in_terms_b, in_terms_a, out_pos, ot_val,
            ot_terms_b, ot_terms_a, grad_agg, w_radial,
        ),
        [pltpu.VMEM((tall, channels), bf16)] * 2
        + [pltpu.VMEM((tall, inner), f32)] * 2
        + [pltpu.VMEM((tall, outer), f32)] * 2
        + [pltpu.VMEM((2, 3, slots, slots), f32), pltpu.VMEM((12, 3, 8, slots), f32)],
    )
    part = total.astype(bf16)
    corner_b = own_acc[0] + add(got_a[rows : rows + channels], got_b[rows : rows + channels])
    corner_a = own_acc[3] + add(got_a[rows + channels :], got_b[rows + channels :])
    sent = lines.astype(bf16)
    got = lax.ppermute(
        jnp.concatenate([part, corner_a.astype(bf16), sent[3 * LINES :]]), "gy", y_even
    )
    far = lax.ppermute(jnp.concatenate([corner_b.astype(bf16), sent[:LINES]]), "gy", y_odd)
    lines_here = lines[LINES : 3 * LINES]
    sent = lines_here.astype(bf16)
    own_b = lax.ppermute(jnp.concatenate([fold_b, sent]), "gx", x_odd)
    own_a = lax.ppermute(jnp.concatenate([fold_a, sent]), "gx", x_even)
    total = add(part, got[:rows])
    step = 2
    while step < len(y_even):
        part = total.astype(bf16)
        got_far = lax.ppermute(part, "gy", across("gy", step))
        total = add(part, got_far)
        step *= 2
    sent = jnp.concatenate([far[channels:], got[rows + channels :]])
    more_b = lax.ppermute(sent, "gx", x_odd)
    more_a = lax.ppermute(sent, "gx", x_even)
    back_a = add(own_a[2 * channels :], more_a)
    back_b = add(own_b[2 * channels :], more_b)
    lines_here = lines_here + sent.astype(f32)
    pos = jnp.concatenate(
        [
            lines_here[base + 4 : base + 8] + (back_a[base : base + 4] + back_b[base + 8 : base + 12])
            for base in (0, LINES)
        ]
    )
    out_feat = call(emit_kernel, 4, shape(features.shape, bf16), (out_here,))
    half = lax.ppermute(total, "gx", x_even)
    grad_feat, grad_pos = call(
        cells_kernel, 4,
        (shape(features.shape, bf16), shape((row_count, 3, col_count, slots), f32)),
        (own_acc, own_a, own_b, far, got, pos, cotangent, w_value, in_gains),
    )
    grad_feat, grad_pos, wvalue, wradial, ggain, wout = call(
        finish_kernel, 4,
        (
            shape(grad_feat.shape, bf16),
            shape(grad_pos.shape, f32),
            shape((channels, channels), f32),
            shape((basis_count, channels), f32),
            shape((type_count, channels), f32),
            shape((channels, channels), f32),
        ),
        (total, half, grad_feat, grad_pos),
    )
    return out_feat, grad_feat, jnp.swapaxes(grad_pos, 1, 2), wvalue, wradial, ggain, wout


def solution(mesh):
    cell = P(("frame", "gx"), "gy", None, None)

    return jax.shard_map(
        on_device,
        mesh=mesh,
        in_specs=(
            cell, cell, P(("frame", "gx"), "gy", None), P(("frame", "gx"), "gy"),
            P(), P(), P(), P(), cell,
        ),
        out_specs=(cell, cell, cell) + (P("frame", None),) * 4,
        check_vma=False,
    )
```

profile of v0, /device:TPU:0, one launch (start us, length us, event | category | flops | bytes accessed | tf_op | source)
XLA Modules:
  0.0 47.1 jit_solution(6672236920116591016)
XLA Ops:
  0.6 0.1 pad_add_fusion.order
  0.7 1.4 %pack.1.own = bf16[2,136,128]{2,1,0:T(8,128)(2,1)S(1)} custom-call(s32[2]{0:T(128)S(1)} %pad_add_fusion.order, s32[1,2]{1,0:T(1,128)} %counts.1, bf16[1,2,128,128]{3,2,1,0:T(8,128)(2,1)} %feat.1, f32[1,3,2,128]{3,2,1,0:T(2,128)} %bitcast.12, s32[1,2,128]{2,1,0:T(2,128)} %types.1), custom_call_target="tpu_custom_call" | custom-call | tf_op jit(solution)/shard_map/pack/pallas_call | solution.py:517
  2.1 2.5 %collective-permute-start.1 = (bf16[2,136,128]{2,1,0:T(8,128)(2,1)S(1)}, bf16[2,136,128]{2,1,0:T(8,128)(2,1)S(1)}, u32[]{:S(2)}, u32[]{:S(2)}) collective-permute-start(bf16[2,136,128]{2,1,0:T(8,128)(2,1)S(1)} %pack.1.own), channel_id=1, source_target_pairs={{0,24},{8,16},{16,8},{24,0},{1,25},{9,17},{17,9},{25,1},{2,26},{10... | collective-permute-start | bytes 208904 | tf_op jit(solution)/shard_map/ppermute | solution.py:541
  4.6 0.7 %collective-permute-start = (bf16[2,136,128]{2,1,0:T(8,128)(2,1)S(1)}, bf16[2,136,128]{2,1,0:T(8,128)(2,1)S(1)}, u32[]{:S(2)}, u32[]{:S(2)}) collective-permute-start(bf16[2,136,128]{2,1,0:T(8,128)(2,1)S(1)} %pack.1.own), channel_id=1, source_target_pairs={{0,8},{8,0},{16,24},{24,16},{1,9},{9,1},{17,25},{25,17},{2,10},{10... | collective-permute-start | bytes 208904 | tf_op jit(solution)/shard_map/ppermute | solution.py:542
  5.3 1.9 %collective-permute-done.1.row_b = bf16[2,136,128]{2,1,0:T(8,128)(2,1)S(1)} collective-permute-done((bf16[2,136,128]{2,1,0:T(8,128)(2,1)S(1)}, bf16[2,136,128]{2,1,0:T(8,128)(2,1)S(1)}, u32[]{:S(2)}, u32[]{:S(2)}) %collective-permute-start.1) | collective-permute-done | bytes 69664 | tf_op jit(solution)/shard_map/ppermute | solution.py:541
  7.2 0.0 collective-permute-done.row_a
  7.2 2.5 %collective-permute-start.2 = (bf16[3,136,128]{2,1,0:T(8,128)(2,1)S(1)}, bf16[3,136,128]{2,1,0:T(8,128)(2,1)S(1)}, u32[]{:S(2)}, u32[]{:S(2)}) collective-permute-start(bf16[3,136,128]{2,1,0:T(8,128)(2,1)S(1)} %pad_maximum_fusion), channel_id=1, source_target_pairs={{0,2},{2,0},{4,6},{6,4},{1,3},{3,1},{5,7},{7,5},{8,10},{10,8},{12,... | collective-permute-start | bytes 313352 | tf_op jit(solution)/shard_map/ppermute | solution.py:544
  9.8 2.5 %collective-permute-start.3 = (bf16[3,136,128]{2,1,0:T(8,128)(2,1)S(1)}, bf16[3,136,128]{2,1,0:T(8,128)(2,1)S(1)}, u32[]{:S(2)}, u32[]{:S(2)}) collective-permute-start(bf16[3,136,128]{2,1,0:T(8,128)(2,1)S(1)} %pad_maximum_fusion.1), channel_id=1, source_target_pairs={{0,6},{2,4},{4,2},{6,0},{1,7},{3,5},{5,3},{7,1},{8,14},{10,12},{12... | collective-permute-start | bytes 313352 | tf_op jit(solution)/shard_map/ppermute | solution.py:543
  12.3 0.9 %load.1 = (bf16[1,2,128,128]{3,2,1,0:T(8,128)(2,1)S(1)}, bf16[128,128]{1,0:T(8,128)(2,1)S(1)}, f32[8,128]{1,0:T(8,128)S(1)}, f32[16,128]{1,0:T(8,128)S(1)}, bf16[128,128]{1,0:T(8,128)(2,1)S(1)}) custom-call(bf16[1,2,128,128]{3,2,1,0:T(8,128)(2,1)} %refs_0_.1, bf16[128,128]{1,0:T(8,128)(2,1)} %refs_1_.1, f32[8,128]{1,0:T(8,128)} %refs_2_.1, ...), custom_call_target="tpu_custom_call" | custom-call | tf_op jit(solution)/shard_map/load/pallas_call | solution.py:532
  13.2 4.3 %shard_map.144 = (f32[6,8,128]{2,1,0:T(8,128)S(1)}, f32[2,3,128,128]{3,2,1,0:T(8,128)S(1)}, bf16[768,128]{1,0:T(8,128)(2,1)S(1)}, bf16[768,128]{1,0:T(8,128)(2,1...) custom-call(s32[2]{0:T(128)S(1)} %pad_add_fusion.order, ...), custom_call_target="tpu_custom_call" | custom-call | tf_op jit(solution)/shard_map/pallas_call | solution.py:502
  17.5 0.0 collective-permute-done.2.col_a
  17.5 0.0 collective-permute-done.3.col_b
  17.5 4.5 %shard_map.145 = (bf16[2,128,128]{2,1,0:T(8,128)(2,1)S(1)}, bf16[144,128]{1,0:T(8,128)(2,1)S(1)}, bf16[400,128]{1,0:T(8,128)(2,1)S(1)}, bf16[400,128]{1,0:T(8,12...) custom-call(s32[2]{0:T(128)S(1)} %pad_add_fusion.order, ...), custom_call_target="tpu_custom_call" | custom-call | tf_op jit(solution)/shard_map/pallas_call | solution.py:502
  22.0 3.9 %shard_map.147 = f32[64,128]{1,0:T(8,128)S(1)} custom-call(s32[2]{0:T(128)S(1)} %pad_add_fusion.order, f32[6,8,128]{2,1,0:T(8,128)S(1)} %get-tuple-element.72.in_pos, f32[2,3,128,128]{3,2,1,0:T(8,128)S(1)} %get-tuple-element.57.own_pos, bf16[768,128]{1,0:T(8,128)(2,1)S(1)} %get-tuple-element.73.in_val, f32[3,128,768]{2,1,0:T(8,128)S(1)} %get-tuple-element.74.in_terms_b, ...), custom_call_target="tpu_custom_call" | custom-call | tf_op jit(solution)/shard_map/pallas_call | solution.py:502
  25.9 0.1 collective-permute-start.4
  26.0 1.7 %collective-permute-start.6 = (bf16[400,128]{1,0:T(8,128)(2,1)S(1)}, bf16[400,128]{1,0:T(8,128)(2,1)S(1)}, u32[]{:S(2)}, u32[]{:S(2)}) collective-permute-start(bf16[400,128]{1,0:T(8,128)(2,1)S(1)} %get-tuple-element.70), channel_id=1, source_target_pairs={{0,24},{8,16},{16,8},{24,0},{1,25},{9,17},{17,9},{25,1},{2,26},{10... | collective-permute-start | bytes 307208 | tf_op jit(solution)/shard_map/ppermute | solution.py:609
  27.7 0.4 collective-permute-start.5
  28.1 0.0 collective-permute-done.4
  28.1 2.6 %collective-permute-done.6 = bf16[400,128]{1,0:T(8,128)(2,1)S(1)} collective-permute-done((bf16[400,128]{1,0:T(8,128)(2,1)S(1)}, bf16[400,128]{1,0:T(8,128)(2,1)S(1)}, u32[]{:S(2)}, u32[]{:S(2)}) %collective-permute-start.6) | collective-permute-done | bytes 102432 | tf_op jit(solution)/shard_map/ppermute | solution.py:609
  30.7 1.5 %collective-permute-start.12 = (bf16[144,128]{1,0:T(8,128)(2,1)S(1)}, bf16[144,128]{1,0:T(8,128)(2,1)S(1)}, u32[]{:S(2)}, u32[]{:S(2)}) collective-permute-start(bf16[144,128]{1,0:T(8,128)(2,1)S(1)} %pad_maximum_fusion.5), channel_id=1, source_target_pairs={{0,6},{2,4},{4,2},{6,0},{1,7},{3,5},{5,3},{7,1},{8,14},{10,12},{12... | collective-permute-start | bytes 110600 | tf_op jit(solution)/shard_map/ppermute | solution.py:639
  32.2 0.0 collective-permute-done.5
  32.3 1.0 %collective-permute-start.7 = (bf16[288,128]{1,0:T(8,128)(2,1)S(1)}, bf16[288,128]{1,0:T(8,128)(2,1)S(1)}, u32[]{:S(2)}, u32[]{:S(2)}) collective-permute-start(bf16[288,128]{1,0:T(8,128)(2,1)S(1)} %pad_maximum_fusion.4), channel_id=1, source_target_pairs={{0,2},{2,0},{4,6},{6,4},{1,3},{3,1},{5,7},{7,5},{8,10},{10,8},{12,... | collective-permute-start | bytes 221192 | tf_op jit(solution)/shard_map/ppermute | solution.py:636
  33.3 1.2 %shard_map.146 = bf16[1,2,128,128]{3,2,1,0:T(8,128)(2,1)} custom-call(s32[2]{0:T(128)S(1)} %pad_add_fusion.order, bf16[2,128,128]{2,1,0:T(8,128)(2,1)S(1)} %get-tuple-element.67.out_here), custom_call_target="tpu_custom_call" | custom-call | tf_op jit(solution)/shard_map/pallas_call | solution.py:502
  34.5 1.3 %collective-permute-start.11 = (bf16[288,128]{1,0:T(8,128)(2,1)S(1)}, bf16[288,128]{1,0:T(8,128)(2,1)S(1)}, u32[]{:S(2)}, u32[]{:S(2)}) collective-permute-start(bf16[288,128]{1,0:T(8,128)(2,1)S(1)} %get-tuple-element.103), channel_id=1, source_target_pairs={{0,24},{8,16},{16,8},{24,0},{1,25},{9,17},{17,9},{25,1},{2,26},{10... | collective-permute-start | bytes 221192 | tf_op jit(solution)/shard_map/ppermute | solution.py:642
  35.8 0.2 collective-permute-start.10
  36.1 0.9 %collective-permute-done.12.far = bf16[144,128]{1,0:T(8,128)(2,1)S(1)} collective-permute-done((bf16[144,128]{1,0:T(8,128)(2,1)S(1)}, bf16[144,128]{1,0:T(8,128)(2,1)S(1)}, u32[]{:S(2)}, u32[]{:S(2)}) %collective-permute-start.12) | collective-permute-done | bytes 36896 | tf_op jit(solution)/shard_map/ppermute | solution.py:639
  37.0 0.8 %collective-permute-done.7.near = bf16[288,128]{1,0:T(8,128)(2,1)S(1)} collective-permute-done((bf16[288,128]{1,0:T(8,128)(2,1)S(1)}, bf16[288,128]{1,0:T(8,128)(2,1)S(1)}, u32[]{:S(2)}, u32[]{:S(2)}) %collective-permute-start.7) | collective-permute-done | bytes 73760 | tf_op jit(solution)/shard_map/ppermute | solution.py:636
  37.8 0.1 collective-permute-start.13
  37.9 1.7 %collective-permute-start.14 = (bf16[32,128]{1,0:T(8,128)(2,1)S(1)}, bf16[32,128]{1,0:T(8,128)(2,1)S(1)}, u32[]{:S(2)}, u32[]{:S(2)}) collective-permute-start(bf16[32,128]{1,0:T(8,128)(2,1)S(1)} %pad_maximum_fusion.6), channel_id=1, source_target_pairs={{0,24},{8,16},{16,8},{24,0},{1,25},{9,17},{17,9},{25,1},{2,26},{10... | collective-permute-start | bytes 24584 | tf_op jit(solution)/shard_map/ppermute | solution.py:652
  39.6 1.2 %collective-permute-start.8 = (bf16[144,128]{1,0:T(8,128)(2,1)S(1)}, bf16[144,128]{1,0:T(8,128)(2,1)S(1)}, u32[]{:S(2)}, u32[]{:S(2)}) collective-permute-start(bf16[144,128]{1,0:T(8,128)(2,1)S(1)} %add_convert_fusion), channel_id=1, source_target_pairs={{0,4},{2,6},{4,0},{6,2},{1,5},{3,7},{5,1},{7,3},{8,12},{10,14},{12... | collective-permute-start | bytes 110600 | tf_op jit(solution)/shard_map/ppermute | solution.py:648
  40.7 0.0 collective-permute-done.10.got_a
  40.7 0.0 collective-permute-done.13
  40.7 0.0 collective-permute-done.11.got_b
  40.7 0.3 collective-permute-done.14
  41.0 3.5 %collective-permute-done.8 = bf16[144,128]{1,0:T(8,128)(2,1)S(1)} collective-permute-done((bf16[144,128]{1,0:T(8,128)(2,1)S(1)}, bf16[144,128]{1,0:T(8,128)(2,1)S(1)}, u32[]{:S(2)}, u32[]{:S(2)}) %collective-permute-start.8) | collective-permute-done | bytes 36896 | tf_op jit(solution)/shard_map/ppermute | solution.py:648
  44.5 0.1 collective-permute-start.9
  44.6 0.8 %shard_map.148 = (bf16[1,2,128,128]{3,2,1,0:T(8,128)(2,1)S(1)}, f32[1,3,2,128]{3,2,1,0:T(2,128)S(1)}) custom-call(s32[2]{0:T(128)S(1)} %pad_add_fusion.order, f32[4,128,128]{2,1,0:T(8,128)S(1)} %get-tuple-element.71.own, bf16[288,128]{1,0:T(8,128)(2,1)S(1)} %collective-permute-done.10.got_a, bf16[288,128]{1,0:T(8,128)(2,1)S(1)} %collective-permute-done.11.got_b, ...), custom_call_target="tpu_custom_call" | custom-call | tf_op jit(solution)/shard_map/pallas_call | solution.py:502
  45.4 0.4 collective-permute-done.9.other
  45.8 1.2 %shard_map.149 = (bf16[1,2,128,128]{3,2,1,0:T(8,128)(2,1)}, f32[1,3,2,128]{3,2,1,0:T(2,128)}, f32[128,128]{1,0:T(8,128)}, f32[8,128]{1,0:T(8,128)}, f32[16,128]{1,0:T(8,128)}, /*index=5*/f32[128,128]{1,0:T(8,128)}) custom-call(s32[2]{0:T(128)S(1)} %pad_add_fusion.order, f32[144,128]{1,0:T(8,128)S(1)} %convert_add_fusion.mine, ...), custom_call_target="tpu_custom_call" | custom-call | tf_op jit(solution)/shard_map/pallas_call | solution.py:502
  (23 shorter events, 0.2 us)
Async XLA Ops:
  2.1 5.1 %collective-permute-start.1 = (bf16[2,136,128]{2,1,0:T(8,128)(2,1)S(1)}, bf16[2,136,128]{2,1,0:T(8,128)(2,1)S(1)}, u32[]{:S(2)}, u32[]{:S(2)}) collective-permute-start(bf16[2,136,128]{2,1,0:T(8,128)(2,1)S(1)} %pack.1.own), channel_id=1, source_target_pairs={{0,24},{8,16},{16,8},{24,0},{1,25},{9,17},{17,9},{25,1},{2,26},{10... | collective-permute-start | bytes 208904 | tf_op jit(solution)/shard_map/ppermute | solution.py:541
  4.6 2.6 %collective-permute-start = (bf16[2,136,128]{2,1,0:T(8,128)(2,1)S(1)}, bf16[2,136,128]{2,1,0:T(8,128)(2,1)S(1)}, u32[]{:S(2)}, u32[]{:S(2)}) collective-permute-start(bf16[2,136,128]{2,1,0:T(8,128)(2,1)S(1)} %pack.1.own), channel_id=1, source_target_pairs={{0,8},{8,0},{16,24},{24,16},{1,9},{9,1},{17,25},{25,17},{2,10},{10... | collective-permute-start | bytes 208904 | tf_op jit(solution)/shard_map/ppermute | solution.py:542
  7.2 10.2 %collective-permute-start.2 = (bf16[3,136,128]{2,1,0:T(8,128)(2,1)S(1)}, bf16[3,136,128]{2,1,0:T(8,128)(2,1)S(1)}, u32[]{:S(2)}, u32[]{:S(2)}) collective-permute-start(bf16[3,136,128]{2,1,0:T(8,128)(2,1)S(1)} %pad_maximum_fusion), channel_id=1, source_target_pairs={{0,2},{2,0},{4,6},{6,4},{1,3},{3,1},{5,7},{7,5},{8,10},{10,8},{12,... | collective-permute-start | bytes 313352 | tf_op jit(solution)/shard_map/ppermute | solution.py:544
  9.8 7.7 %collective-permute-start.3 = (bf16[3,136,128]{2,1,0:T(8,128)(2,1)S(1)}, bf16[3,136,128]{2,1,0:T(8,128)(2,1)S(1)}, u32[]{:S(2)}, u32[]{:S(2)}) collective-permute-start(bf16[3,136,128]{2,1,0:T(8,128)(2,1)S(1)} %pad_maximum_fusion.1), channel_id=1, source_target_pairs={{0,6},{2,4},{4,2},{6,0},{1,7},{3,5},{5,3},{7,1},{8,14},{10,12},{12... | collective-permute-start | bytes 313352 | tf_op jit(solution)/shard_map/ppermute | solution.py:543
  25.9 2.2 %collective-permute-start.4 = (bf16[400,128]{1,0:T(8,128)(2,1)S(1)}, bf16[400,128]{1,0:T(8,128)(2,1)S(1)}, u32[]{:S(2)}, u32[]{:S(2)}) collective-permute-start(bf16[400,128]{1,0:T(8,128)(2,1)S(1)} %get-tuple-element.69), channel_id=1, source_target_pairs={{0,8},{8,0},{16,24},{24,16},{1,9},{9,1},{17,25},{25,17},{2,10},{10... | collective-permute-start | bytes 307208 | tf_op jit(solution)/shard_map/ppermute | solution.py:610
  26.0 4.7 %collective-permute-start.6 = (bf16[400,128]{1,0:T(8,128)(2,1)S(1)}, bf16[400,128]{1,0:T(8,128)(2,1)S(1)}, u32[]{:S(2)}, u32[]{:S(2)}) collective-permute-start(bf16[400,128]{1,0:T(8,128)(2,1)S(1)} %get-tuple-element.70), channel_id=1, source_target_pairs={{0,24},{8,16},{16,8},{24,0},{1,25},{9,17},{17,9},{25,1},{2,26},{10... | collective-permute-start | bytes 307208 | tf_op jit(solution)/shard_map/ppermute | solution.py:609
  27.7 4.6 %collective-permute-start.5 = (bf16[144,128]{1,0:T(8,128)(2,1)S(1)}, bf16[144,128]{1,0:T(8,128)(2,1)S(1)}, u32[]{:S(2)}, u32[]{:S(2)}) collective-permute-start(bf16[144,128]{1,0:T(8,128)(2,1)S(1)} %get-tuple-element.68), channel_id=1, source_target_pairs={{0,16},{8,24},{16,0},{24,8},{1,17},{9,25},{17,1},{25,9},{2,18},{10... | collective-permute-start | bytes 110600 | tf_op jit(solution)/shard_map/ppermute | solution.py:612
  30.7 6.2 %collective-permute-start.12 = (bf16[144,128]{1,0:T(8,128)(2,1)S(1)}, bf16[144,128]{1,0:T(8,128)(2,1)S(1)}, u32[]{:S(2)}, u32[]{:S(2)}) collective-permute-start(bf16[144,128]{1,0:T(8,128)(2,1)S(1)} %pad_maximum_fusion.5), channel_id=1, source_target_pairs={{0,6},{2,4},{4,2},{6,0},{1,7},{3,5},{5,3},{7,1},{8,14},{10,12},{12... | collective-permute-start | bytes 110600 | tf_op jit(solution)/shard_map/ppermute | solution.py:639
  32.3 5.5 %collective-permute-start.7 = (bf16[288,128]{1,0:T(8,128)(2,1)S(1)}, bf16[288,128]{1,0:T(8,128)(2,1)S(1)}, u32[]{:S(2)}, u32[]{:S(2)}) collective-permute-start(bf16[288,128]{1,0:T(8,128)(2,1)S(1)} %pad_maximum_fusion.4), channel_id=1, source_target_pairs={{0,2},{2,0},{4,6},{6,4},{1,3},{3,1},{5,7},{7,5},{8,10},{10,8},{12,... | collective-permute-start | bytes 221192 | tf_op jit(solution)/shard_map/ppermute | solution.py:636
  34.5 6.3 %collective-permute-start.11 = (bf16[288,128]{1,0:T(8,128)(2,1)S(1)}, bf16[288,128]{1,0:T(8,128)(2,1)S(1)}, u32[]{:S(2)}, u32[]{:S(2)}) collective-permute-start(bf16[288,128]{1,0:T(8,128)(2,1)S(1)} %get-tuple-element.103), channel_id=1, source_target_pairs={{0,24},{8,16},{16,8},{24,0},{1,25},{9,17},{17,9},{25,1},{2,26},{10... | collective-permute-start | bytes 221192 | tf_op jit(solution)/shard_map/ppermute | solution.py:642
  35.8 4.9 %collective-permute-start.10 = (bf16[288,128]{1,0:T(8,128)(2,1)S(1)}, bf16[288,128]{1,0:T(8,128)(2,1)S(1)}, u32[]{:S(2)}, u32[]{:S(2)}) collective-permute-start(bf16[288,128]{1,0:T(8,128)(2,1)S(1)} %get-tuple-element.104), channel_id=1, source_target_pairs={{0,8},{8,0},{16,24},{24,16},{1,9},{9,1},{17,25},{25,17},{2,10},{10... | collective-permute-start | bytes 221192 | tf_op jit(solution)/shard_map/ppermute | solution.py:643
  37.8 2.9 %collective-permute-start.13 = (bf16[32,128]{1,0:T(8,128)(2,1)S(1)}, bf16[32,128]{1,0:T(8,128)(2,1)S(1)}, u32[]{:S(2)}, u32[]{:S(2)}) collective-permute-start(bf16[32,128]{1,0:T(8,128)(2,1)S(1)} %pad_maximum_fusion.6), channel_id=1, source_target_pairs={{0,8},{8,0},{16,24},{24,16},{1,9},{9,1},{17,25},{25,17},{2,10},{10... | collective-permute-start | bytes 24584 | tf_op jit(solution)/shard_map/ppermute | solution.py:653
  37.9 3.1 %collective-permute-start.14 = (bf16[32,128]{1,0:T(8,128)(2,1)S(1)}, bf16[32,128]{1,0:T(8,128)(2,1)S(1)}, u32[]{:S(2)}, u32[]{:S(2)}) collective-permute-start(bf16[32,128]{1,0:T(8,128)(2,1)S(1)} %pad_maximum_fusion.6), channel_id=1, source_target_pairs={{0,24},{8,16},{16,8},{24,0},{1,25},{9,17},{17,9},{25,1},{2,26},{10... | collective-permute-start | bytes 24584 | tf_op jit(solution)/shard_map/ppermute | solution.py:652
  39.6 4.9 %collective-permute-start.8 = (bf16[144,128]{1,0:T(8,128)(2,1)S(1)}, bf16[144,128]{1,0:T(8,128)(2,1)S(1)}, u32[]{:S(2)}, u32[]{:S(2)}) collective-permute-start(bf16[144,128]{1,0:T(8,128)(2,1)S(1)} %add_convert_fusion), channel_id=1, source_target_pairs={{0,4},{2,6},{4,0},{6,2},{1,5},{3,7},{5,1},{7,3},{8,12},{10,14},{12... | collective-permute-start | bytes 110600 | tf_op jit(solution)/shard_map/ppermute | solution.py:648
  44.5 1.3 %collective-permute-start.9 = (f32[144,128]{1,0:T(8,128)S(1)}, f32[144,128]{1,0:T(8,128)S(1)}, u32[]{:S(2)}, u32[]{:S(2)}) collective-permute-start(f32[144,128]{1,0:T(8,128)S(1)} %convert_add_fusion.mine), channel_id=1, source_target_pairs={{0,8},{8,0},{16,24},{24,16},{1,9},{9,1},{17,25},{25,17},{2,10},{10... | collective-permute-start | bytes 221192 | tf_op jit(solution)/shard_map/ppermute | solution.py:664
where the time goes:
time: 47.3 us; the launch traced here: 47.1 us
  Pallas kernels  18.1 us (38%)
  starting transfers between devices  17.5 us (37%)
  waiting for transfers between devices  10.4 us (22%)
  between operations  0.82 us (2%)
    pallas_call x6, Pallas kernels, call(): pl.pallas_call(kernel, out_shape=out_shape, in_specs=[smem] + [vmem] * le...  15.8 us
    ppermute x1, waiting for transfers between devices, on_device(): got_far = lax.ppermute(part, 'gy', across('gy', step))  3.46 us
    ppermute x1, waiting for transfers between devices, on_device(): got_b = lax.ppermute(pay_b, 'gx', x_odd)  2.61 us
    ppermute x1, starting transfers between devices, on_device(): lax.ppermute(jnp.stack([row_a[0], packed[0], row_b[0]]), 'gy', y_odd)  2.54 us
    ppermute x1, starting transfers between devices, on_device(): lax.ppermute(jnp.stack([row_a[1], packed[1], row_b[1]]), 'gy', y_even)  2.52 us
    ppermute x1, starting transfers between devices, on_device(): row_b = lax.ppermute(packed, 'gx', x_odd)  2.5 us
    ppermute x1, waiting for transfers between devices, on_device(): row_b = lax.ppermute(packed, 'gx', x_odd)  1.89 us
    ppermute x1, starting transfers between devices, on_device(): got_b = lax.ppermute(pay_b, 'gx', x_odd)  1.69 us
  transfers between devices with their start and end apart: 15, of which 7 were waited for; matrix products, arithmetic and copies ran while one was open for 0% of the time, Pallas kernels for 15%

commit v1 on v0

--- a/solution.py
+++ b/solution.py
@@ -431,7 +431,7 @@
 
 
 def cells_kernel(
-    order, own, got_a, got_b, far, near, lines, cotangent, w_value, gains, grad_feat, grad_pos
+    order, own, got_a, got_b, far, near, cotangent, w_value, gains, grad_feat
 ):
     slots = own.shape[2]
     for place in range(2):
@@ -441,9 +441,6 @@
         total = own[place + 1] + add(got_a[here, :], got_b[here, :]) + got.astype(f32)
         half = (total * gains[:, (3 * place + 1) * slots : (3 * place + 2) * slots]).astype(bf16)
         grad_feat[0, cell] = (cotangent[0, cell].astype(f32) + dot(w_value[...], half).T).astype(bf16)
-        pos = lines[4 * place : 4 * place + 4, :]
-        for comp in range(3):
-            grad_pos[0, comp, pl.ds(cell, 1), :] = pos[comp : comp + 1]
 
 
 def emit_kernel(order, out_here, out_feat):
@@ -451,9 +448,13 @@
         out_feat[0, jnp.where(order[1] == 0, place, 1 - place)] = out_here[place]
 
 
-def finish_kernel(order, mine, other, feat, pos, grad_feat, grad_pos, wvalue, wradial, ggain, wout):
+def finish_kernel(order, mine, other, feat, lines, grad_feat, grad_pos, wvalue, wradial, ggain, wout):
     grad_feat[...] = feat[...]
-    grad_pos[...] = pos[...]
+    for place in range(2):
+        cell = jnp.where(order[1] == 0, place, 1 - place)
+        for comp in range(3):
+            row = 4 * place + comp
+            grad_pos[0, comp, pl.ds(cell, 1), :] = lines[row : row + 1, :]
     first = order[0] == 0
     low = jnp.where(first, mine[...], other[...])
     high = jnp.where(first, other[...], mine[...])
@@ -662,22 +663,21 @@
     )
     out_feat = call(emit_kernel, 4, shape(features.shape, bf16), (out_here,))
     half = lax.ppermute(total, "gx", x_even)
-    grad_feat, grad_pos = call(
-        cells_kernel, 4,
-        (shape(features.shape, bf16), shape((row_count, 3, col_count, slots), f32)),
-        (own_acc, own_a, own_b, far, got, pos, cotangent, w_value, in_gains),
+    grad_feat = call(
+        cells_kernel, 4, shape(features.shape, bf16),
+        (own_acc, own_a, own_b, far, got, cotangent, w_value, in_gains),
     )
     grad_feat, grad_pos, wvalue, wradial, ggain, wout = call(
         finish_kernel, 4,
         (
             shape(grad_feat.shape, bf16),
-            shape(grad_pos.shape, f32),
+            shape((row_count, 3, col_count, slots), f32),
             shape((channels, channels), f32),
             shape((basis_count, channels), f32),
             shape((type_count, channels), f32),
             shape((channels, channels), f32),
         ),
-        (total, half, grad_feat, grad_pos),
+        (total, half, grad_feat, pos),
     )
     return out_feat, grad_feat, jnp.swapaxes(grad_pos, 1, 2), wvalue, wradial, ggain, wout
 

time: 47.3 us -> 47.3 us (level)
    ppermute x1, waiting for transfers between devices: 0.42 us -> 1.24 us  [on_device(): half = lax.ppermute(total, 'gx', x_even)]
    ppermute x1, waiting for transfers between devices: 3.46 us -> 2.92 us  [on_device(): got_far = lax.ppermute(part, 'gy', across('gy', step))]
  transfers between devices with their start and end apart: 15 -> 15, of which waited for: 7 -> 6; matrix products, arithmetic and copies ran while one was open for 0% -> 0% of each run, Pallas kernels for 15% -> 15%
where the time goes in v1:
time: 47.3 us; the launch traced here: 47.1 us
  Pallas kernels  18.1 us (38%)
  starting transfers between devices  17.5 us (37%)
  waiting for transfers between devices  10.3 us (22%)
  between operations  0.83 us (2%)
    pallas_call x6, Pallas kernels, call(): pl.pallas_call(kernel, out_shape=out_shape, in_specs=[smem] + [vmem] * le...  15.8 us
    ppermute x1, waiting for transfers between devices, on_device(): got_far = lax.ppermute(part, 'gy', across('gy', step))  2.92 us
    ppermute x1, waiting for transfers between devices, on_device(): got_b = lax.ppermute(pay_b, 'gx', x_odd)  2.58 us
    ppermute x1, starting transfers between devices, on_device(): lax.ppermute(jnp.stack([row_a[0], packed[0], row_b[0]]), 'gy', y_odd)  2.54 us
    ppermute x1, starting transfers between devices, on_device(): lax.ppermute(jnp.stack([row_a[1], packed[1], row_b[1]]), 'gy', y_even)  2.52 us
    ppermute x1, starting transfers between devices, on_device(): row_b = lax.ppermute(packed, 'gx', x_odd)  2.5 us
    ppermute x1, waiting for transfers between devices, on_device(): row_b = lax.ppermute(packed, 'gx', x_odd)  1.89 us
    ppermute x1, starting transfers between devices, on_device(): more_b = lax.ppermute(sent, 'gx', x_odd)  1.68 us
  transfers between devices with their start and end apart: 15, of which 6 were waited for; matrix products, arithmetic and copies ran while one was open for 0% of the time, Pallas kernels for 15%

profile of v1, /device:TPU:0, one launch (start us, length us, event | category | flops | bytes accessed | tf_op | source)
XLA Modules:
  0.0 47.1 jit_solution(6696911422568295088)
XLA Ops:
  0.6 0.1 pad_add_fusion.order
  0.7 1.4 %pack.1.own = bf16[2,136,128]{2,1,0:T(8,128)(2,1)S(1)} custom-call(s32[2]{0:T(128)S(1)} %pad_add_fusion.order, s32[1,2]{1,0:T(1,128)} %counts.1, bf16[1,2,128,128]{3,2,1,0:T(8,128)(2,1)} %feat.1, f32[1,3,2,128]{3,2,1,0:T(2,128)} %bitcast.12, s32[1,2,128]{2,1,0:T(2,128)} %types.1), custom_call_target="tpu_custom_call" | custom-call | tf_op jit(solution)/shard_map/pack/pallas_call | solution.py:518
  2.1 2.5 %collective-permute-start.1 = (bf16[2,136,128]{2,1,0:T(8,128)(2,1)S(1)}, bf16[2,136,128]{2,1,0:T(8,128)(2,1)S(1)}, u32[]{:S(2)}, u32[]{:S(2)}) collective-permute-start(bf16[2,136,128]{2,1,0:T(8,128)(2,1)S(1)} %pack.1.own), channel_id=1, source_target_pairs={{0,24},{8,16},{16,8},{24,0},{1,25},{9,17},{17,9},{25,1},{2,26},{10... | collective-permute-start | bytes 208904 | tf_op jit(solution)/shard_map/ppermute | solution.py:542
  4.6 0.7 %collective-permute-start = (bf16[2,136,128]{2,1,0:T(8,128)(2,1)S(1)}, bf16[2,136,128]{2,1,0:T(8,128)(2,1)S(1)}, u32[]{:S(2)}, u32[]{:S(2)}) collective-permute-start(bf16[2,136,128]{2,1,0:T(8,128)(2,1)S(1)} %pack.1.own), channel_id=1, source_target_pairs={{0,8},{8,0},{16,24},{24,16},{1,9},{9,1},{17,25},{25,17},{2,10},{10... | collective-permute-start | bytes 208904 | tf_op jit(solution)/shard_map/ppermute | solution.py:543
  5.3 1.9 %collective-permute-done.1.row_b = bf16[2,136,128]{2,1,0:T(8,128)(2,1)S(1)} collective-permute-done((bf16[2,136,128]{2,1,0:T(8,128)(2,1)S(1)}, bf16[2,136,128]{2,1,0:T(8,128)(2,1)S(1)}, u32[]{:S(2)}, u32[]{:S(2)}) %collective-permute-start.1) | collective-permute-done | bytes 69664 | tf_op jit(solution)/shard_map/ppermute | solution.py:542
  7.2 0.0 collective-permute-done.row_a
  7.2 2.5 %collective-permute-start.2 = (bf16[3,136,128]{2,1,0:T(8,128)(2,1)S(1)}, bf16[3,136,128]{2,1,0:T(8,128)(2,1)S(1)}, u32[]{:S(2)}, u32[]{:S(2)}) collective-permute-start(bf16[3,136,128]{2,1,0:T(8,128)(2,1)S(1)} %pad_maximum_fusion), channel_id=1, source_target_pairs={{0,2},{2,0},{4,6},{6,4},{1,3},{3,1},{5,7},{7,5},{8,10},{10,8},{12,... | collective-permute-start | bytes 313352 | tf_op jit(solution)/shard_map/ppermute | solution.py:545
  9.8 2.5 %collective-permute-start.3 = (bf16[3,136,128]{2,1,0:T(8,128)(2,1)S(1)}, bf16[3,136,128]{2,1,0:T(8,128)(2,1)S(1)}, u32[]{:S(2)}, u32[]{:S(2)}) collective-permute-start(bf16[3,136,128]{2,1,0:T(8,128)(2,1)S(1)} %pad_maximum_fusion.1), channel_id=1, source_target_pairs={{0,6},{2,4},{4,2},{6,0},{1,7},{3,5},{5,3},{7,1},{8,14},{10,12},{12... | collective-permute-start | bytes 313352 | tf_op jit(solution)/shard_map/ppermute | solution.py:544
  12.3 0.9 %load.1 = (bf16[1,2,128,128]{3,2,1,0:T(8,128)(2,1)S(1)}, bf16[128,128]{1,0:T(8,128)(2,1)S(1)}, f32[8,128]{1,0:T(8,128)S(1)}, f32[16,128]{1,0:T(8,128)S(1)}, bf16[128,128]{1,0:T(8,128)(2,1)S(1)}) custom-call(bf16[1,2,128,128]{3,2,1,0:T(8,128)(2,1)} %refs_0_.1, bf16[128,128]{1,0:T(8,128)(2,1)} %refs_1_.1, f32[8,128]{1,0:T(8,128)} %refs_2_.1, ...), custom_call_target="tpu_custom_call" | custom-call | tf_op jit(solution)/shard_map/load/pallas_call | solution.py:533
  13.2 4.3 %shard_map.144 = (f32[6,8,128]{2,1,0:T(8,128)S(1)}, f32[2,3,128,128]{3,2,1,0:T(8,128)S(1)}, bf16[768,128]{1,0:T(8,128)(2,1)S(1)}, bf16[768,128]{1,0:T(8,128)(2,1...) custom-call(s32[2]{0:T(128)S(1)} %pad_add_fusion.order, ...), custom_call_target="tpu_custom_call" | custom-call | tf_op jit(solution)/shard_map/pallas_call | solution.py:503
  17.5 0.0 collective-permute-done.2.col_a
  17.5 0.0 collective-permute-done.3.col_b
  17.5 4.5 %shard_map.145 = (bf16[2,128,128]{2,1,0:T(8,128)(2,1)S(1)}, bf16[144,128]{1,0:T(8,128)(2,1)S(1)}, bf16[400,128]{1,0:T(8,128)(2,1)S(1)}, bf16[400,128]{1,0:T(8,12...) custom-call(s32[2]{0:T(128)S(1)} %pad_add_fusion.order, ...), custom_call_target="tpu_custom_call" | custom-call | tf_op jit(solution)/shard_map/pallas_call | solution.py:503
  22.0 3.9 %shard_map.147 = f32[64,128]{1,0:T(8,128)S(1)} custom-call(s32[2]{0:T(128)S(1)} %pad_add_fusion.order, f32[6,8,128]{2,1,0:T(8,128)S(1)} %get-tuple-element.70.in_pos, f32[2,3,128,128]{3,2,1,0:T(8,128)S(1)} %get-tuple-element.55.own_pos, bf16[768,128]{1,0:T(8,128)(2,1)S(1)} %get-tuple-element.71.in_val, f32[3,128,768]{2,1,0:T(8,128)S(1)} %get-tuple-element.72.in_terms_b, ...), custom_call_target="tpu_custom_call" | custom-call | tf_op jit(solution)/shard_map/pallas_call | solution.py:503
  25.9 0.1 collective-permute-start.4
  26.0 1.7 %collective-permute-start.6 = (bf16[400,128]{1,0:T(8,128)(2,1)S(1)}, bf16[400,128]{1,0:T(8,128)(2,1)S(1)}, u32[]{:S(2)}, u32[]{:S(2)}) collective-permute-start(bf16[400,128]{1,0:T(8,128)(2,1)S(1)} %get-tuple-element.68), channel_id=1, source_target_pairs={{0,24},{8,16},{16,8},{24,0},{1,25},{9,17},{17,9},{25,1},{2,26},{10... | collective-permute-start | bytes 307208 | tf_op jit(solution)/shard_map/ppermute | solution.py:610
  27.6 0.5 %collective-permute-start.5 = (bf16[144,128]{1,0:T(8,128)(2,1)S(1)}, bf16[144,128]{1,0:T(8,128)(2,1)S(1)}, u32[]{:S(2)}, u32[]{:S(2)}) collective-permute-start(bf16[144,128]{1,0:T(8,128)(2,1)S(1)} %get-tuple-element.66), channel_id=1, source_target_pairs={{0,16},{8,24},{16,0},{24,8},{1,17},{9,25},{17,1},{25,9},{2,18},{10... | collective-permute-start | bytes 110600 | tf_op jit(solution)/shard_map/ppermute | solution.py:613
  28.1 0.0 collective-permute-done.4
  28.1 2.6 %collective-permute-done.6 = bf16[400,128]{1,0:T(8,128)(2,1)S(1)} collective-permute-done((bf16[400,128]{1,0:T(8,128)(2,1)S(1)}, bf16[400,128]{1,0:T(8,128)(2,1)S(1)}, u32[]{:S(2)}, u32[]{:S(2)}) %collective-permute-start.6) | collective-permute-done | bytes 102432 | tf_op jit(solution)/shard_map/ppermute | solution.py:610
  30.7 1.5 %collective-permute-start.12 = (bf16[144,128]{1,0:T(8,128)(2,1)S(1)}, bf16[144,128]{1,0:T(8,128)(2,1)S(1)}, u32[]{:S(2)}, u32[]{:S(2)}) collective-permute-start(bf16[144,128]{1,0:T(8,128)(2,1)S(1)} %pad_maximum_fusion.5), channel_id=1, source_target_pairs={{0,6},{2,4},{4,2},{6,0},{1,7},{3,5},{5,3},{7,1},{8,14},{10,12},{12... | collective-permute-start | bytes 110600 | tf_op jit(solution)/shard_map/ppermute | solution.py:640
  32.2 0.0 collective-permute-done.5
  32.3 1.0 %collective-permute-start.7 = (bf16[288,128]{1,0:T(8,128)(2,1)S(1)}, bf16[288,128]{1,0:T(8,128)(2,1)S(1)}, u32[]{:S(2)}, u32[]{:S(2)}) collective-permute-start(bf16[288,128]{1,0:T(8,128)(2,1)S(1)} %pad_maximum_fusion.4), channel_id=1, source_target_pairs={{0,2},{2,0},{4,6},{6,4},{1,3},{3,1},{5,7},{7,5},{8,10},{10,8},{12,... | collective-permute-start | bytes 221192 | tf_op jit(solution)/shard_map/ppermute | solution.py:637
  33.3 1.2 %shard_map.146 = bf16[1,2,128,128]{3,2,1,0:T(8,128)(2,1)} custom-call(s32[2]{0:T(128)S(1)} %pad_add_fusion.order, bf16[2,128,128]{2,1,0:T(8,128)(2,1)S(1)} %get-tuple-element.65.out_here), custom_call_target="tpu_custom_call" | custom-call | tf_op jit(solution)/shard_map/pallas_call | solution.py:503
  34.5 1.3 %collective-permute-start.11 = (bf16[288,128]{1,0:T(8,128)(2,1)S(1)}, bf16[288,128]{1,0:T(8,128)(2,1)S(1)}, u32[]{:S(2)}, u32[]{:S(2)}) collective-permute-start(bf16[288,128]{1,0:T(8,128)(2,1)S(1)} %get-tuple-element.99), channel_id=1, source_target_pairs={{0,24},{8,16},{16,8},{24,0},{1,25},{9,17},{17,9},{25,1},{2,26},{10... | collective-permute-start | bytes 221192 | tf_op jit(solution)/shard_map/ppermute | solution.py:643
  35.8 0.2 collective-permute-start.10
  36.1 0.9 %collective-permute-done.12.far = bf16[144,128]{1,0:T(8,128)(2,1)S(1)} collective-permute-done((bf16[144,128]{1,0:T(8,128)(2,1)S(1)}, bf16[144,128]{1,0:T(8,128)(2,1)S(1)}, u32[]{:S(2)}, u32[]{:S(2)}) %collective-permute-start.12) | collective-permute-done | bytes 36896 | tf_op jit(solution)/shard_map/ppermute | solution.py:640
  36.9 0.8 %collective-permute-done.7.near = bf16[288,128]{1,0:T(8,128)(2,1)S(1)} collective-permute-done((bf16[288,128]{1,0:T(8,128)(2,1)S(1)}, bf16[288,128]{1,0:T(8,128)(2,1)S(1)}, u32[]{:S(2)}, u32[]{:S(2)}) %collective-permute-start.7) | collective-permute-done | bytes 73760 | tf_op jit(solution)/shard_map/ppermute | solution.py:637
  37.8 0.1 collective-permute-start.13
  37.9 1.7 %collective-permute-start.14 = (bf16[32,128]{1,0:T(8,128)(2,1)S(1)}, bf16[32,128]{1,0:T(8,128)(2,1)S(1)}, u32[]{:S(2)}, u32[]{:S(2)}) collective-permute-start(bf16[32,128]{1,0:T(8,128)(2,1)S(1)} %pad_maximum_fusion.6), channel_id=1, source_target_pairs={{0,24},{8,16},{16,8},{24,0},{1,25},{9,17},{17,9},{25,1},{2,26},{10... | collective-permute-start | bytes 24584 | tf_op jit(solution)/shard_map/ppermute | solution.py:653
  39.6 1.1 %collective-permute-start.8 = (bf16[144,128]{1,0:T(8,128)(2,1)S(1)}, bf16[144,128]{1,0:T(8,128)(2,1)S(1)}, u32[]{:S(2)}, u32[]{:S(2)}) collective-permute-start(bf16[144,128]{1,0:T(8,128)(2,1)S(1)} %add_convert_fusion), channel_id=1, source_target_pairs={{0,4},{2,6},{4,0},{6,2},{1,5},{3,7},{5,1},{7,3},{8,12},{10,14},{12... | collective-permute-start | bytes 110600 | tf_op jit(solution)/shard_map/ppermute | solution.py:649
  40.7 0.0 collective-permute-done.11.got_b
  40.7 0.0 collective-permute-done.10.got_a
  40.7 0.8 %shard_map.148.feat = bf16[1,2,128,128]{3,2,1,0:T(8,128)(2,1)S(1)} custom-call(s32[2]{0:T(128)S(1)} %pad_add_fusion.order, f32[4,128,128]{2,1,0:T(8,128)S(1)} %get-tuple-element.69.own, bf16[288,128]{1,0:T(8,128)(2,1)S(1)} %collective-permute-done.10.got_a, bf16[288,128]{1,0:T(8,128)(2,1)S(1)} %collective-permute-done.11.got_b, ...), custom_call_target="tpu_custom_call" | custom-call | tf_op jit(solution)/shard_map/pallas_call | solution.py:503
  41.5 0.0 collective-permute-done.13
  41.5 0.0 collective-permute-done.14
  41.6 2.9 %collective-permute-done.8 = bf16[144,128]{1,0:T(8,128)(2,1)S(1)} collective-permute-done((bf16[144,128]{1,0:T(8,128)(2,1)S(1)}, bf16[144,128]{1,0:T(8,128)(2,1)S(1)}, u32[]{:S(2)}, u32[]{:S(2)}) %collective-permute-start.8) | collective-permute-done | bytes 36896 | tf_op jit(solution)/shard_map/ppermute | solution.py:649
  44.5 0.1 collective-permute-start.9
  44.6 1.2 %collective-permute-done.9.other = f32[144,128]{1,0:T(8,128)S(1)} collective-permute-done((f32[144,128]{1,0:T(8,128)S(1)}, f32[144,128]{1,0:T(8,128)S(1)}, u32[]{:S(2)}, u32[]{:S(2)}) %collective-permute-start.9) | collective-permute-done | bytes 73760 | tf_op jit(solution)/shard_map/ppermute | solution.py:665
  45.8 1.2 %shard_map.149 = (bf16[1,2,128,128]{3,2,1,0:T(8,128)(2,1)}, f32[1,3,2,128]{3,2,1,0:T(2,128)}, f32[128,128]{1,0:T(8,128)}, f32[8,128]{1,0:T(8,128)}, f32[16,128]{1,0:T(8,128)}, /*index=5*/f32[128,128]{1,0:T(8,128)}) custom-call(s32[2]{0:T(128)S(1)} %pad_add_fusion.order, f32[144,128]{1,0:T(8,128)S(1)} %convert_add_fusion.mine, ...), custom_call_target="tpu_custom_call" | custom-call | tf_op jit(solution)/shard_map/pallas_call | solution.py:503
  (23 shorter events, 0.2 us)
Async XLA Ops:
  2.1 5.1 %collective-permute-start.1 = (bf16[2,136,128]{2,1,0:T(8,128)(2,1)S(1)}, bf16[2,136,128]{2,1,0:T(8,128)(2,1)S(1)}, u32[]{:S(2)}, u32[]{:S(2)}) collective-permute-start(bf16[2,136,128]{2,1,0:T(8,128)(2,1)S(1)} %pack.1.own), channel_id=1, source_target_pairs={{0,24},{8,16},{16,8},{24,0},{1,25},{9,17},{17,9},{25,1},{2,26},{10... | collective-permute-start | bytes 208904 | tf_op jit(solution)/shard_map/ppermute | solution.py:542
  4.6 2.6 %collective-permute-start = (bf16[2,136,128]{2,1,0:T(8,128)(2,1)S(1)}, bf16[2,136,128]{2,1,0:T(8,128)(2,1)S(1)}, u32[]{:S(2)}, u32[]{:S(2)}) collective-permute-start(bf16[2,136,128]{2,1,0:T(8,128)(2,1)S(1)} %pack.1.own), channel_id=1, source_target_pairs={{0,8},{8,0},{16,24},{24,16},{1,9},{9,1},{17,25},{25,17},{2,10},{10... | collective-permute-start | bytes 208904 | tf_op jit(solution)/shard_map/ppermute | solution.py:543
  7.2 10.2 %collective-permute-start.2 = (bf16[3,136,128]{2,1,0:T(8,128)(2,1)S(1)}, bf16[3,136,128]{2,1,0:T(8,128)(2,1)S(1)}, u32[]{:S(2)}, u32[]{:S(2)}) collective-permute-start(bf16[3,136,128]{2,1,0:T(8,128)(2,1)S(1)} %pad_maximum_fusion), channel_id=1, source_target_pairs={{0,2},{2,0},{4,6},{6,4},{1,3},{3,1},{5,7},{7,5},{8,10},{10,8},{12,... | collective-permute-start | bytes 313352 | tf_op jit(solution)/shard_map/ppermute | solution.py:545
  9.8 7.7 %collective-permute-start.3 = (bf16[3,136,128]{2,1,0:T(8,128)(2,1)S(1)}, bf16[3,136,128]{2,1,0:T(8,128)(2,1)S(1)}, u32[]{:S(2)}, u32[]{:S(2)}) collective-permute-start(bf16[3,136,128]{2,1,0:T(8,128)(2,1)S(1)} %pad_maximum_fusion.1), channel_id=1, source_target_pairs={{0,6},{2,4},{4,2},{6,0},{1,7},{3,5},{5,3},{7,1},{8,14},{10,12},{12... | collective-permute-start | bytes 313352 | tf_op jit(solution)/shard_map/ppermute | solution.py:544
  25.9 2.2 %collective-permute-start.4 = (bf16[400,128]{1,0:T(8,128)(2,1)S(1)}, bf16[400,128]{1,0:T(8,128)(2,1)S(1)}, u32[]{:S(2)}, u32[]{:S(2)}) collective-permute-start(bf16[400,128]{1,0:T(8,128)(2,1)S(1)} %get-tuple-element.67), channel_id=1, source_target_pairs={{0,8},{8,0},{16,24},{24,16},{1,9},{9,1},{17,25},{25,17},{2,10},{10... | collective-permute-start | bytes 307208 | tf_op jit(solution)/shard_map/ppermute | solution.py:611
  26.0 4.7 %collective-permute-start.6 = (bf16[400,128]{1,0:T(8,128)(2,1)S(1)}, bf16[400,128]{1,0:T(8,128)(2,1)S(1)}, u32[]{:S(2)}, u32[]{:S(2)}) collective-permute-start(bf16[400,128]{1,0:T(8,128)(2,1)S(1)} %get-tuple-element.68), channel_id=1, source_target_pairs={{0,24},{8,16},{16,8},{24,0},{1,25},{9,17},{17,9},{25,1},{2,26},{10... | collective-permute-start | bytes 307208 | tf_op jit(solution)/shard_map/ppermute | solution.py:610
  27.6 4.6 %collective-permute-start.5 = (bf16[144,128]{1,0:T(8,128)(2,1)S(1)}, bf16[144,128]{1,0:T(8,128)(2,1)S(1)}, u32[]{:S(2)}, u32[]{:S(2)}) collective-permute-start(bf16[144,128]{1,0:T(8,128)(2,1)S(1)} %get-tuple-element.66), channel_id=1, source_target_pairs={{0,16},{8,24},{16,0},{24,8},{1,17},{9,25},{17,1},{25,9},{2,18},{10... | collective-permute-start | bytes 110600 | tf_op jit(solution)/shard_map/ppermute | solution.py:613
  30.7 6.2 %collective-permute-start.12 = (bf16[144,128]{1,0:T(8,128)(2,1)S(1)}, bf16[144,128]{1,0:T(8,128)(2,1)S(1)}, u32[]{:S(2)}, u32[]{:S(2)}) collective-permute-start(bf16[144,128]{1,0:T(8,128)(2,1)S(1)} %pad_maximum_fusion.5), channel_id=1, source_target_pairs={{0,6},{2,4},{4,2},{6,0},{1,7},{3,5},{5,3},{7,1},{8,14},{10,12},{12... | collective-permute-start | bytes 110600 | tf_op jit(solution)/shard_map/ppermute | solution.py:640
  32.3 5.5 %collective-permute-start.7 = (bf16[288,128]{1,0:T(8,128)(2,1)S(1)}, bf16[288,128]{1,0:T(8,128)(2,1)S(1)}, u32[]{:S(2)}, u32[]{:S(2)}) collective-permute-start(bf16[288,128]{1,0:T(8,128)(2,1)S(1)} %pad_maximum_fusion.4), channel_id=1, source_target_pairs={{0,2},{2,0},{4,6},{6,4},{1,3},{3,1},{5,7},{7,5},{8,10},{10,8},{12,... | collective-permute-start | bytes 221192 | tf_op jit(solution)/shard_map/ppermute | solution.py:637
  34.5 6.2 %collective-permute-start.11 = (bf16[288,128]{1,0:T(8,128)(2,1)S(1)}, bf16[288,128]{1,0:T(8,128)(2,1)S(1)}, u32[]{:S(2)}, u32[]{:S(2)}) collective-permute-start(bf16[288,128]{1,0:T(8,128)(2,1)S(1)} %get-tuple-element.99), channel_id=1, source_target_pairs={{0,24},{8,16},{16,8},{24,0},{1,25},{9,17},{17,9},{25,1},{2,26},{10... | collective-permute-start | bytes 221192 | tf_op jit(solution)/shard_map/ppermute | solution.py:643
  35.8 4.9 %collective-permute-start.10 = (bf16[288,128]{1,0:T(8,128)(2,1)S(1)}, bf16[288,128]{1,0:T(8,128)(2,1)S(1)}, u32[]{:S(2)}, u32[]{:S(2)}) collective-permute-start(bf16[288,128]{1,0:T(8,128)(2,1)S(1)} %get-tuple-element.100), channel_id=1, source_target_pairs={{0,8},{8,0},{16,24},{24,16},{1,9},{9,1},{17,25},{25,17},{2,10},{10... | collective-permute-start | bytes 221192 | tf_op jit(solution)/shard_map/ppermute | solution.py:644
  37.8 3.7 %collective-permute-start.13 = (bf16[32,128]{1,0:T(8,128)(2,1)S(1)}, bf16[32,128]{1,0:T(8,128)(2,1)S(1)}, u32[]{:S(2)}, u32[]{:S(2)}) collective-permute-start(bf16[32,128]{1,0:T(8,128)(2,1)S(1)} %pad_maximum_fusion.6), channel_id=1, source_target_pairs={{0,8},{8,0},{16,24},{24,16},{1,9},{9,1},{17,25},{25,17},{2,10},{10... | collective-permute-start | bytes 24584 | tf_op jit(solution)/shard_map/ppermute | solution.py:654
  37.9 3.7 %collective-permute-start.14 = (bf16[32,128]{1,0:T(8,128)(2,1)S(1)}, bf16[32,128]{1,0:T(8,128)(2,1)S(1)}, u32[]{:S(2)}, u32[]{:S(2)}) collective-permute-start(bf16[32,128]{1,0:T(8,128)(2,1)S(1)} %pad_maximum_fusion.6), channel_id=1, source_target_pairs={{0,24},{8,16},{16,8},{24,0},{1,25},{9,17},{17,9},{25,1},{2,26},{10... | collective-permute-start | bytes 24584 | tf_op jit(solution)/shard_map/ppermute | solution.py:653
  39.6 4.9 %collective-permute-start.8 = (bf16[144,128]{1,0:T(8,128)(2,1)S(1)}, bf16[144,128]{1,0:T(8,128)(2,1)S(1)}, u32[]{:S(2)}, u32[]{:S(2)}) collective-permute-start(bf16[144,128]{1,0:T(8,128)(2,1)S(1)} %add_convert_fusion), channel_id=1, source_target_pairs={{0,4},{2,6},{4,0},{6,2},{1,5},{3,7},{5,1},{7,3},{8,12},{10,14},{12... | collective-permute-start | bytes 110600 | tf_op jit(solution)/shard_map/ppermute | solution.py:649
  44.5 1.3 %collective-permute-start.9 = (f32[144,128]{1,0:T(8,128)S(1)}, f32[144,128]{1,0:T(8,128)S(1)}, u32[]{:S(2)}, u32[]{:S(2)}) collective-permute-start(f32[144,128]{1,0:T(8,128)S(1)} %convert_add_fusion.mine), channel_id=1, source_target_pairs={{0,8},{8,0},{16,24},{24,16},{1,9},{9,1},{17,25},{25,17},{2,10},{10... | collective-permute-start | bytes 221192 | tf_op jit(solution)/shard_map/ppermute | solution.py:665
